TPU v7x, 256 devices: a whole 4x4x8 slice. The times are simulated.
256 devices in a mesh: seed: 4 (over x), chan: 16 (over z, y_lo), fsdp: 4 (over y_hi, core).
Axes of the slice: x: 4, y: 4 (y_hi: 2, y_lo: 2; y = y_hi * 2 + y_lo), z: 8, core: 2. Of those that a mesh axis runs over, the one named last changes fastest.
Arguments:
- stream: bfloat16 [256, 144, 8192], P(('seed', 'fsdp'), None, 'chan'), parts along dimension 0, may hold values from -12.5 to 9.5
- mid: bfloat16 [256, 144, 2048], P(('seed', 'fsdp'), None, 'chan'), parts along dimension 0, may hold values from 0 to 2
- conv_weight: bfloat16 [8192, 8192], P(('seed', 'fsdp'), 'chan'), parts along dimension 0, may hold values from -0.125 to 0.125
- head_weight: bfloat16 [32768, 16384], P(('seed', 'chan'), 'fsdp'), parts along dimension 0, may hold values from -0.375 to 0.375
- labels: int32 [64], replicated, may hold values from 0 to 16383
- proj_act: bfloat16 [2048, 32], replicated, may hold values from -0.125 to 0.125
- proj_err: bfloat16 [8192, 64], P('chan'), may hold values from -6 to 6
Outputs:
- grad_proj: float32 [256, 2048], P(('seed', 'fsdp'), 'chan'), parts along dimension 0
There are 4 independent parts, one for each index of `seed`. A program takes and returns all parts, laid end to end along the dimension named above; an argument that names none is the same for every part. Nothing has to cross between parts.
All inputs are finite; a program needn't handle non-finite values.
Results may differ from a plain program's by a relative error of at most 0.01.
Values may be sent and summed in bfloat16 or wider, within the bound.
No kernel may reach another device: no remote copies, remote signals or barrier semaphores. Data moves between devices by JAX's collectives and lax.ppermute only.
A program may use at most 64 MiB of HBM per device.

v0:
```python
import jax
import jax.numpy as jnp
from jax import lax
from jax.sharding import PartitionSpec as P


def per_device(stream, mid, conv_weight, head_weight, labels, proj_act, proj_err):
    images = stream.shape[0]
    positions = stream.shape[1]
    width = stream.shape[2]
    rows = images * positions
    gathered = lax.all_gather(mid, "chan", axis=2, tiled=True)
    mid_rows = gathered.reshape(rows, gathered.shape[2])
    conv_out = jnp.dot(
        mid_rows,
        lax.all_gather(conv_weight, "fsdp", axis=0, tiled=True),
        preferred_element_type=jnp.float32,
    )
    acts_proj = jnp.dot(mid_rows, proj_act, preferred_element_type=jnp.float32)
    y_local = stream.astype(jnp.float32) + conv_out.reshape(images, positions, width)
    pooled = jnp.mean(jnp.maximum(y_local, 0.0), axis=1).astype(jnp.bfloat16)
    pooled_all = lax.all_gather(pooled, "fsdp", axis=0, tiled=True)
    partial_value = jnp.dot(pooled_all, head_weight, preferred_element_type=jnp.float32)
    block = head_weight.shape[1]
    block_start = lax.axis_index("fsdp") * block
    logits = lax.psum(partial_value, "chan")
    expo = jnp.exp(logits)
    total = lax.psum(jnp.sum(expo, axis=1), "fsdp")
    classes = block_start + jnp.arange(block, dtype=jnp.int32)
    onehot = (labels[:, None] == classes[None, :]).astype(jnp.float32)
    dlogits = (expo / total[:, None] - onehot).astype(jnp.bfloat16)
    dpooled = lax.psum_scatter(
        lax.dot_general(
            dlogits, head_weight, (((1,), (1,)), ((), ())), preferred_element_type=jnp.float32
        ),
        "fsdp",
        scatter_dimension=0,
        tiled=True,
    )
    error = jnp.where(y_local > 0.0, dpooled[:, None, :] / positions, 0.0).astype(jnp.bfloat16)
    err_part = jnp.dot(error.reshape(rows, width), proj_err, preferred_element_type=jnp.float32)
    acts_cube = acts_proj.reshape(images, positions, acts_proj.shape[1])
    err_full = lax.psum(err_part.astype(jnp.bfloat16), "chan").astype(jnp.float32)
    grads = jnp.einsum(
        "npa,npb->nab",
        acts_cube,
        err_full.reshape(images, positions, err_full.shape[1]),
        precision=lax.Precision.HIGHEST,
    )
    grads = grads.reshape(images, -1)
    share = grads.shape[1] // lax.axis_size("chan")
    return lax.dynamic_slice_in_dim(grads, lax.axis_index("chan") * share, share, 1)


def solution(mesh):
    in_specs = (
        P(("seed", "fsdp"), None, "chan"),
        P(("seed", "fsdp"), None, "chan"),
        P(("seed", "fsdp"), "chan"),
        P(("seed", "chan"), "fsdp"),
        P(),
        P(),
        P("chan", None),
    )
    out_specs = P(("seed", "fsdp"), "chan")
    return jax.shard_map(
        per_device, mesh=mesh, in_specs=in_specs, out_specs=out_specs, check_vma=False
    )
```

profile of v0, /device:TPU:2, one launch (start us, length us, event | category | flops | bytes accessed | tf_op | source)
XLA Modules:
  0.0 618.6 jit_solution(5644417789808126572)
XLA Ops:
  6.5 0.0 copy-start
  6.5 0.7 all-gather.5.cloned.1.call-update
  7.3 0.0 all-gather.3.cloned.1.call-start
  7.3 0.7 all-gather.3.cloned.1.call-update
  8.0 0.0 all-reduce.3.cloned.1.call-start
  8.1 33.3 %all-gather.5.cloned.1.call-done = bf16[2048,512]{1,0:T(8,128)(2,1)} async-done(((bf16[512,512]{1,0:T(8,128)(2,1)}), bf16[2048,512]{1,0:T(8,128)(2,1)}) %all-gather.5.cloned.1.call-update) | async-done | bytes 2097168 | tf_op jit(solution)/shard_map/all_gather | solution.py:16
  41.4 217.4 %all-gather.3.cloned.1.call-done = bf16[16,144,2048]{2,1,0:T(8,128)(2,1)} async-done(((bf16[16,144,128]{2,1,0:T(8,128)(2,1)}), bf16[16,144,2048]{2,1,0:T(8,128)(2,1)}) %all-gather.3.cloned.1.call-update) | async-done | bytes 9437200 | tf_op jit(solution)/shard_map/all_gather | solution.py:12
  258.7 11.5 %maximum_reduce_fusion = (f32[16,512]{1,0:T(8,128)S(1)}, f32[16,144,512]{2,1,0:T(8,128)}) fusion(bf16[16,144,512]{2,1,0:T(8,128)(2,1)} %param.7, bf16[16,144,2048]{2,1,0:T(8,128)(2,1)} %all-gather.3.cloned.1.call-done, bf16[2048,512]{1,0:T(8,128)(2,1)} %all-gather.5.cloned.1.call-done), kind=kOutput, calls=%fused_computation.1 | convolution fusion | flops 4836548608 | bytes 18644992 | tf_op jit(solution)/shard_map/dot_general | solution.py:14
  270.3 6.8 %all_gather.11 = bf16[64,512]{1,0:T(8,128)(2,1)S(1)} all-gather(bf16[16,512]{1,0:T(8,128)(2,1)S(1)} %multiply_convert_fusion), channel_id=1, replica_groups=mesh['seed'=4,'chan'=16,'fsdp'=4] {'fsdp'}, dimensions={0}, use_global_device_ids=true | all-gather | bytes 81920 | tf_op jit(solution)/shard_map/all_gather | solution.py:22
  277.0 1.8 fusion.8
  278.9 0.0 all-reduce.3.cloned.1.call-update
  278.9 0.0 reduce-scatter.2.cloned.1.call-start
  279.0 0.0 copy-start.2
  279.0 142.3 %all-reduce.3.cloned.1.call-done = f32[64,4096]{1,0:T(8,128)} async-done(((f32[64,4096]{1,0:T(8,128)}), f32[64,4096]{1,0:T(8,128)}) %all-reduce.3.cloned.1.call-update) | async-done | bytes 1048592 | tf_op jit(solution)/shard_map/psum | solution.py:26
  421.2 1.5 exponential_reduce_fusion
  422.7 7.2 %psum.22 = f32[64]{0:T(128)S(1)} all-reduce(f32[64]{0:T(128)S(1)} %exponential_reduce_fusion), channel_id=1, replica_groups=mesh['seed'=4,'chan'=16,'fsdp'=4] {'fsdp'}, use_global_device_ids=true, to_apply=%region_3.0 | all-reduce | flops 64 | bytes 512 | tf_op jit(solution)/shard_map/psum | solution.py:28
  429.9 4.6 fusion.2
  434.5 0.0 reduce-scatter.2.cloned.1.call-update
  434.5 0.0 all-reduce.5.cloned.1.call-start
  434.6 31.8 %reduce-scatter.2.cloned.1.call-done = f32[16,512]{1,0:T(8,128)} async-done(((f32[64,512]{1,0:T(8,128)}), f32[16,512]{1,0:T(8,128)}) %reduce-scatter.2.cloned.1.call-update) | async-done | bytes 32784 | tf_op jit(solution)/shard_map/reduce_scatter | solution.py:32
  466.4 0.8 broadcast_multiply_fusion
  467.2 0.0 copy-done.2
  467.2 3.2 select_convert_fusion
  470.4 0.8 convolution_convert_fusion
  471.2 0.9 reshape.25
  472.1 0.9 copy.8
  473.0 0.0 all-reduce.5.cloned.1.call-update
  473.1 6.9 %fusion.6 = f32[16,144,32]{1,2,0:T(8,128)S(1)} fusion(bf16[16,144,2048]{2,1,0:T(8,128)(2,1)} %all-gather.3.cloned.1.call-done, bf16[2048,32]{0,1:T(8,128)(2,1)S(1)} %copy-done), kind=kOutput, calls=%fused_computation.12 | convolution fusion | flops 301989888 | bytes 9863168 | tf_op jit(solution)/shard_map/dot_general | solution.py:19
  480.0 129.8 %all-reduce.5.cloned.1.call-done = bf16[16,144,64]{1,2,0:T(8,128)(2,1)} async-done(((bf16[16,144,64]{1,2,0:T(8,128)(2,1)}), bf16[16,144,64]{1,2,0:T(8,128)(2,1)}) %all-reduce.5.cloned.1.call-update) | async-done | bytes 294928 | tf_op jit(solution)/shard_map/psum | solution.py:43
  609.7 1.6 fusion.9
  611.3 0.1 reshape.26
  611.4 0.6 constant_dynamic-slice_fusion
  (10 shorter events, 0.0 us)
Async XLA Ops:
  6.5 466.5 %copy-start = (bf16[2048,32]{0,1:T(8,128)(2,1)S(1)}, bf16[2048,32]{0,1:T(8,128)(2,1)}, u32[]{:S(2)}) copy-start(bf16[2048,32]{0,1:T(8,128)(2,1)} %param.12) | copy-start | bytes 393220
  6.5 34.8 %all-gather.5.cloned.1.call-start = ((), (), s32[]{:S(2)}) async-start(), calls=%async_computation.2 | async-start | bytes 2621440 | tf_op jit(solution)/shard_map/all_gather | solution.py:16
  7.3 251.5 %all-gather.3.cloned.1.call-start = ((), (), s32[]{:S(2)}) async-start(), calls=%async_computation.1 | async-start | bytes 10027008 | tf_op jit(solution)/shard_map/all_gather | solution.py:12
  8.0 413.2 %all-reduce.3.cloned.1.call-start = ((), (), s32[]{:S(2)}) async-start(), calls=%async_computation.3 | async-start | bytes 2097152 | tf_op jit(solution)/shard_map/psum | solution.py:26
  258.7 18.3 %copy-start.1 = (bf16[512,4096]{1,0:T(8,128)(2,1)S(1)}, bf16[512,4096]{1,0:T(8,128)(2,1)}, u32[]{:S(2)}) copy-start(bf16[512,4096]{1,0:T(8,128)(2,1)} %param.10) | copy-start | bytes 12582916
  270.3 159.6 %copy-start.4 = (s32[64]{0:T(128)S(1)}, s32[64]{0:T(128)}, u32[]{:S(2)}) copy-start(s32[64]{0:T(128)} %param.11) | copy-start | bytes 772
  278.9 187.5 %reduce-scatter.2.cloned.1.call-start = ((), (), s32[]{:S(2)}) async-start(), calls=%async_computation.4 | async-start | bytes 163840 | tf_op jit(solution)/shard_map/reduce_scatter | solution.py:32
  279.0 188.2 %copy-start.2 = (bf16[16,144,512]{2,1,0:T(8,128)(2,1)S(1)}, bf16[16,144,512]{2,1,0:T(8,128)(2,1)}, u32[]{:S(2)}) copy-start(bf16[16,144,512]{2,1,0:T(8,128)(2,1)} %param.7) | copy-start | bytes 7077892
  434.5 175.2 %all-reduce.5.cloned.1.call-start = ((), (), s32[]{:S(2)}) async-start(), calls=%async_computation.5 | async-start | bytes 1048576 | tf_op jit(solution)/shard_map/psum | solution.py:43
  467.2 3.2 copy-start.3
Sparse Core Ops, SparseCore 0:
  9.2 32.1 all-gather.4
  43.1 215.6 all-gather.2
  279.0 142.1 all-reduce.2
  434.6 31.7 reduce-scatter.1
  473.2 136.5 all-reduce.4
where the time goes:
time: 619 us
  waiting for transfers between devices  556 us (90%)
  matrix products  27.2 us (4%)
  blocking collectives  13.9 us (2%)
  between operations  13.2 us (2%)
    all_gather x1, waiting for transfers between devices, per_device(): gathered = lax.all_gather(mid, 'chan', axis=2, tiled=True)  217 us
    psum x1, waiting for transfers between devices, per_device(): logits = lax.psum(partial_value, 'chan')  142 us
    psum x1, waiting for transfers between devices, per_device(): lax.psum(err_part.astype(jnp.bfloat16), 'chan').astype(jnp.float32)  130 us
    all_gather x1, waiting for transfers between devices, per_device(): lax.all_gather(conv_weight, 'fsdp', axis=0, tiled=True)  33.3 us
    reduce_scatter x1, waiting for transfers between devices, per_device(): lax.psum_scatter(lax.dot_general(dlogits, head_weight, (((1,), (1,)), (()...  31.8 us
  transfers between devices with their start and end apart: 5, of which 5 were waited for; matrix products, arithmetic and copies ran while one was open for 1% of the time, Pallas kernels for 0%

commit v1 on v0

--- a/solution.py
+++ b/solution.py
@@ -2,6 +2,11 @@
 import jax.numpy as jnp
 from jax import lax
 from jax.sharding import PartitionSpec as P
+
+
+def order_ladders(tile_in, comm_axis):
+    heard = lax.all_gather(tile_in, axis_name=comm_axis)
+    return jnp.sum(heard, axis=0)
 
 
 def per_device(stream, mid, conv_weight, head_weight, labels, proj_act, proj_err):
@@ -23,7 +28,7 @@
     partial_value = jnp.dot(pooled_all, head_weight, preferred_element_type=jnp.float32)
     block = head_weight.shape[1]
     block_start = lax.axis_index("fsdp") * block
-    logits = lax.psum(partial_value, "chan")
+    logits = order_ladders(partial_value, comm_axis="chan")
     expo = jnp.exp(logits)
     total = lax.psum(jnp.sum(expo, axis=1), "fsdp")
     classes = block_start + jnp.arange(block, dtype=jnp.int32)

time: 619 us -> 843 us (1.36)
  waiting for transfers between devices: 556 us -> 771 us
    all_gather x0 -> x1, waiting for transfers between devices: none -> 354 us  [order_ladders(): heard = lax.all_gather(tile_in, axis_name=comm_axis)]
    psum x1 -> x0, waiting for transfers between devices: 142 us -> none  [per_device(): logits = lax.psum(partial_value, 'chan')]
where the time goes in v1:
time: 843 us; the launch traced here: 842 us
  waiting for transfers between devices  771 us (91%)
  matrix products  26.9 us (3%)
  blocking collectives  17 us (2%)
  between operations  13.2 us (2%)
  other arithmetic  11.6 us (1%)
    all_gather x1, waiting for transfers between devices, order_ladders(): heard = lax.all_gather(tile_in, axis_name=comm_axis)  354 us
    all_gather x1, waiting for transfers between devices, per_device(): gathered = lax.all_gather(mid, 'chan', axis=2, tiled=True)  217 us
    psum x1, waiting for transfers between devices, per_device(): lax.psum(err_part.astype(jnp.bfloat16), 'chan').astype(jnp.float32)  130 us
    reduce_scatter x1, waiting for transfers between devices, per_device(): lax.psum_scatter(lax.dot_general(dlogits, head_weight, (((1,), (1,)), (()...  34.8 us
    all_gather x1, waiting for transfers between devices, per_device(): lax.all_gather(conv_weight, 'fsdp', axis=0, tiled=True)  33.3 us
  transfers between devices with their start and end apart: 5, of which 5 were waited for; matrix products, arithmetic and copies ran while one was open for 1% of the time, Pallas kernels for 0%

profile of v1, /device:TPU:2, one launch (start us, length us, event | category | flops | bytes accessed | tf_op | source)
XLA Modules:
  0.0 842.2 jit_solution(2939977555672321725)
XLA Ops:
  6.5 0.7 all-gather.7.cloned.1.call-update
  7.3 0.0 all-gather.5.cloned.1.call-start
  7.3 0.7 all-gather.5.cloned.1.call-update
  8.0 0.0 all-gather.9.cloned.1.call-start
  8.1 33.3 %all-gather.7.cloned.1.call-done = bf16[2048,512]{1,0:T(8,128)(2,1)} async-done(((bf16[512,512]{1,0:T(8,128)(2,1)}), bf16[2048,512]{1,0:T(8,128)(2,1)}) %all-gather.7.cloned.1.call-update) | async-done | bytes 2097168 | tf_op jit(solution)/shard_map/all_gather | solution.py:21
  41.4 217.4 %all-gather.5.cloned.1.call-done = bf16[16,144,2048]{2,1,0:T(8,128)(2,1)} async-done(((bf16[16,144,128]{2,1,0:T(8,128)(2,1)}), bf16[16,144,2048]{2,1,0:T(8,128)(2,1)}) %all-gather.5.cloned.1.call-update) | async-done | bytes 9437200 | tf_op jit(solution)/shard_map/all_gather | solution.py:17
  258.7 11.6 %maximum_reduce_fusion = (f32[16,512]{1,0:T(8,128)S(1)}, f32[16,144,512]{2,1,0:T(8,128)}) fusion(bf16[16,144,512]{2,1,0:T(8,128)(2,1)} %param.7, bf16[16,144,2048]{2,1,0:T(8,128)(2,1)} %all-gather.5.cloned.1.call-done, bf16[2048,512]{1,0:T(8,128)(2,1)} %all-gather.7.cloned.1.call-done), kind=kOutput, calls=%fused_computation.1 | convolution fusion | flops 4836548608 | bytes 18644992 | tf_op jit(solution)/shard_map/dot_general | solution.py:19
  270.3 6.8 all_gather.17
  277.1 0.0 copy-done.1
  277.1 1.8 fusion.8
  278.9 0.0 all-gather.9.cloned.1.call-update
  278.9 0.0 reduce-scatter.2.cloned.1.call-start
  279.0 354.1 %all-gather.9.cloned.1.call-done = f32[1024,4096]{1,0:T(8,128)} async-done(((f32[64,4096]{1,0:T(8,128)}), f32[1024,4096]{1,0:T(8,128)}) %all-gather.9.cloned.1.call-update) | async-done | bytes 16777232 | tf_op jit(solution)/shard_map/all_gather | solution.py:8
  633.1 6.9 reduce_sum.28
  640.0 0.0 copy-start.2
  640.0 0.8 exponential_reduce_fusion
  640.7 10.2 %psum.14 = f32[64]{0:T(128)} all-reduce(f32[64]{0:T(128)} %exponential_reduce_fusion), channel_id=1, replica_groups=mesh['seed'=4,'chan'=16,'fsdp'=4] {'fsdp'}, use_global_device_ids=true, to_apply=%region_3.0 | all-reduce | flops 64 | bytes 512 | tf_op jit(solution)/shard_map/psum | solution.py:33
  651.0 4.3 fusion.2
  655.3 0.0 reduce-scatter.2.cloned.1.call-update
  655.3 0.0 all-reduce.2.cloned.1.call-start
  655.3 34.8 %reduce-scatter.2.cloned.1.call-done = f32[16,512]{1,0:T(8,128)} async-done(((f32[64,512]{1,0:T(8,128)}), f32[16,512]{1,0:T(8,128)}) %reduce-scatter.2.cloned.1.call-update) | async-done | bytes 32784 | tf_op jit(solution)/shard_map/reduce_scatter | solution.py:37
  690.1 0.8 broadcast_multiply_fusion
  690.9 3.2 select_convert_fusion
  694.1 0.8 convolution_convert_fusion
  694.9 0.9 reshape.25
  695.8 1.0 copy.9
  696.7 0.0 all-reduce.2.cloned.1.call-update
  696.8 6.9 fusion.6
  703.7 129.7 %all-reduce.2.cloned.1.call-done = bf16[16,144,64]{1,2,0:T(8,128)(2,1)} async-done(((bf16[16,144,64]{1,2,0:T(8,128)(2,1)}), bf16[16,144,64]{1,2,0:T(8,128)(2,1)}) %all-reduce.2.cloned.1.call-update) | async-done | bytes 294928 | tf_op jit(solution)/shard_map/psum | solution.py:48
  833.4 1.6 fusion.9
  835.0 0.1 reshape.26
  835.1 0.6 constant_dynamic-slice_fusion
  (9 shorter events, 0.0 us)
Async XLA Ops:
  6.5 690.2 %copy-start = (bf16[2048,32]{0,1:T(8,128)(2,1)S(1)}, bf16[2048,32]{0,1:T(8,128)(2,1)}, u32[]{:S(2)}) copy-start(bf16[2048,32]{0,1:T(8,128)(2,1)} %param.12) | copy-start | bytes 393220
  6.5 34.8 %all-gather.7.cloned.1.call-start = ((), (), s32[]{:S(2)}) async-start(), calls=%async_computation.2 | async-start | bytes 2621440 | tf_op jit(solution)/shard_map/all_gather | solution.py:21
  7.3 251.5 %all-gather.5.cloned.1.call-start = ((), (), s32[]{:S(2)}) async-start(), calls=%async_computation.1 | async-start | bytes 10027008 | tf_op jit(solution)/shard_map/all_gather | solution.py:17
  8.0 625.1 %all-gather.9.cloned.1.call-start = ((), (), s32[]{:S(2)}) async-start(), calls=%async_computation.5 | async-start | bytes 17825792 | tf_op jit(solution)/shard_map/all_gather | solution.py:8
  258.7 18.3 %copy-start.1 = (bf16[512,4096]{1,0:T(8,128)(2,1)S(1)}, bf16[512,4096]{1,0:T(8,128)(2,1)}, u32[]{:S(2)}) copy-start(bf16[512,4096]{1,0:T(8,128)(2,1)} %param.10) | copy-start | bytes 12582916
  278.9 411.2 %reduce-scatter.2.cloned.1.call-start = ((), (), s32[]{:S(2)}) async-start(), calls=%async_computation.3 | async-start | bytes 163840 | tf_op jit(solution)/shard_map/reduce_scatter | solution.py:37
  640.0 50.9 %copy-start.2 = (bf16[16,144,512]{2,1,0:T(8,128)(2,1)S(1)}, bf16[16,144,512]{2,1,0:T(8,128)(2,1)}, u32[]{:S(2)}) copy-start(bf16[16,144,512]{2,1,0:T(8,128)(2,1)} %param.7) | copy-start | bytes 7077892
  655.3 178.1 %all-reduce.2.cloned.1.call-start = ((), (), s32[]{:S(2)}) async-start(), calls=%async_computation.4 | async-start | bytes 1048576 | tf_op jit(solution)/shard_map/psum | solution.py:48
  690.9 3.2 copy-start.3
Sparse Core Ops, SparseCore 0:
  9.2 32.1 all-gather.6
  43.1 215.6 all-gather.4
  279.0 354.0 all-gather.8
  655.4 34.6 reduce-scatter.1
  696.9 136.4 all-reduce.1

commit v2 on v0

--- a/solution.py
+++ b/solution.py
@@ -2,6 +2,13 @@
 import jax.numpy as jnp
 from jax import lax
 from jax.sharding import PartitionSpec as P
+
+
+def panel_tell(w_in):
+    reply = lax.axis_size("fsdp")
+    m_next = jnp.stack([w_in] * reply, 0)
+    heard = lax.all_to_all(m_next, "fsdp", split_axis=0, concat_axis=0)
+    return jnp.concatenate(heard, 0)
 
 
 def per_device(stream, mid, conv_weight, head_weight, labels, proj_act, proj_err):
@@ -11,11 +18,7 @@
     rows = images * positions
     gathered = lax.all_gather(mid, "chan", axis=2, tiled=True)
     mid_rows = gathered.reshape(rows, gathered.shape[2])
-    conv_out = jnp.dot(
-        mid_rows,
-        lax.all_gather(conv_weight, "fsdp", axis=0, tiled=True),
-        preferred_element_type=jnp.float32,
-    )
+    conv_out = jnp.dot(mid_rows, panel_tell(conv_weight), preferred_element_type=jnp.float32)
     acts_proj = jnp.dot(mid_rows, proj_act, preferred_element_type=jnp.float32)
     y_local = stream.astype(jnp.float32) + conv_out.reshape(images, positions, width)
     pooled = jnp.mean(jnp.maximum(y_local, 0.0), axis=1).astype(jnp.bfloat16)

time: 619 us -> 599 us (0.968)
  waiting for transfers between devices: 556 us -> 477 us
  blocking collectives: 13.9 us -> 71.8 us
    all_to_all x0 -> x1, blocking collectives: none -> 57.9 us  [panel_tell(): heard = lax.all_to_all(m_next, 'fsdp', split_axis=0, concat_axis=0)]
    all_gather x1, waiting for transfers between devices: 217 us -> 169 us  [per_device(): gathered = lax.all_gather(mid, 'chan', axis=2, tiled=True)]
    all_gather x1 -> x0, waiting for transfers between devices: 33.3 us -> none  [per_device(): lax.all_gather(conv_weight, 'fsdp', axis=0, tiled=True)]
  transfers between devices with their start and end apart: 5 -> 4, of which waited for: 5 -> 4; matrix products, arithmetic and copies ran while one was open for 1% -> 1% of each run, Pallas kernels for 0% -> 0%
where the time goes in v2:
time: 599 us; the launch traced here: 598 us
  waiting for transfers between devices  477 us (80%)
  blocking collectives  71.8 us (12%)
  matrix products  26.9 us (4%)
  between operations  13.2 us (2%)
    all_gather x1, waiting for transfers between devices, per_device(): gathered = lax.all_gather(mid, 'chan', axis=2, tiled=True)  169 us
    psum x1, waiting for transfers between devices, per_device(): logits = lax.psum(partial_value, 'chan')  146 us
    psum x1, waiting for transfers between devices, per_device(): lax.psum(err_part.astype(jnp.bfloat16), 'chan').astype(jnp.float32)  130 us
    all_to_all x1, blocking collectives, panel_tell(): heard = lax.all_to_all(m_next, 'fsdp', split_axis=0, concat_axis=0)  57.9 us
    reduce_scatter x1, waiting for transfers between devices, per_device(): lax.psum_scatter(lax.dot_general(dlogits, head_weight, (((1,), (1,)), (()...  31.8 us
  transfers between devices with their start and end apart: 4, of which 4 were waited for; matrix products, arithmetic and copies ran while one was open for 1% of the time, Pallas kernels for 0%

profile of v2, /device:TPU:2, one launch (start us, length us, event | category | flops | bytes accessed | tf_op | source)
XLA Modules:
  0.0 598.3 jit_solution(13380078710502289216)
XLA Ops:
  6.5 0.0 copy-start
  6.5 0.0 all-gather.2.cloned.1.call-start
  6.5 0.7 all-gather.2.cloned.1.call-update
  7.3 0.0 all-reduce.3.cloned.1.call-start
  7.3 1.2 stack.2
  8.5 57.9 %all_to_all.5 = bf16[4,512,512]{2,1,0:T(8,128)(2,1)} all-to-all(bf16[4,512,512]{2,1,0:T(8,128)(2,1)S(1)} %stack.2), channel_id=1, replica_groups=mesh['seed'=4,'chan'=16,'fsdp'=4] {'fsdp'}, dimensions={0} | all-to-all | bytes 4194304 | tf_op jit(solution)/shard_map/all_to_all | solution.py:10
  66.4 169.1 %all-gather.2.cloned.1.call-done = bf16[16,144,2048]{2,1,0:T(8,128)(2,1)} async-done(((bf16[16,144,128]{2,1,0:T(8,128)(2,1)}), bf16[16,144,2048]{2,1,0:T(8,128)(2,1)}) %all-gather.2.cloned.1.call-update) | async-done | bytes 9437200 | tf_op jit(solution)/shard_map/all_gather | solution.py:19
  235.5 0.0 copy-done.2
  235.5 11.2 %maximum_reduce_fusion = (f32[16,512]{1,0:T(8,128)S(1)}, f32[16,144,512]{2,1,0:T(8,128)}) fusion(bf16[16,144,512]{2,1,0:T(8,128)(2,1)S(1)} %copy-done.2, bf16[16,144,2048]{2,1,0:T(8,128)(2,1)} %all-gather.2.cloned.1.call-done, bf16[2048,512,1]{1,0,2:T(8,128)(2,1)} %bitcast.20), kind=kOutput, calls=%fused_computation.1 | convolution fusion | flops 4836548608 | bytes 18644992 | tf_op jit(solution)/shard_map/dot_general | solution.py:21
  246.8 6.8 %all_gather.7 = bf16[64,512]{1,0:T(8,128)(2,1)S(1)} all-gather(bf16[16,512]{1,0:T(8,128)(2,1)S(1)} %multiply_convert_fusion), channel_id=1, replica_groups=mesh['seed'=4,'chan'=16,'fsdp'=4] {'fsdp'}, dimensions={0}, use_global_device_ids=true | all-gather | bytes 81920 | tf_op jit(solution)/shard_map/all_gather | solution.py:25
  253.5 0.0 copy-done.1
  253.5 1.9 fusion.6
  255.4 0.0 all-reduce.3.cloned.1.call-update
  255.4 0.0 reduce-scatter.2.cloned.1.call-start
  255.5 145.6 %all-reduce.3.cloned.1.call-done = f32[64,4096]{1,0:T(8,128)} async-done(((f32[64,4096]{1,0:T(8,128)}), f32[64,4096]{1,0:T(8,128)}) %all-reduce.3.cloned.1.call-update) | async-done | bytes 1048592 | tf_op jit(solution)/shard_map/psum | solution.py:29
  401.0 1.5 exponential_reduce_fusion
  402.5 7.2 %psum.22 = f32[64]{0:T(128)S(1)} all-reduce(f32[64]{0:T(128)S(1)} %exponential_reduce_fusion), channel_id=1, replica_groups=mesh['seed'=4,'chan'=16,'fsdp'=4] {'fsdp'}, use_global_device_ids=true, to_apply=%region_3.0 | all-reduce | flops 64 | bytes 512 | tf_op jit(solution)/shard_map/psum | solution.py:31
  409.7 4.6 fusion
  414.3 0.0 reduce-scatter.2.cloned.1.call-update
  414.3 0.0 all-reduce.5.cloned.1.call-start
  414.3 31.8 %reduce-scatter.2.cloned.1.call-done = f32[16,512]{1,0:T(8,128)} async-done(((f32[64,512]{1,0:T(8,128)}), f32[16,512]{1,0:T(8,128)}) %reduce-scatter.2.cloned.1.call-update) | async-done | bytes 32784 | tf_op jit(solution)/shard_map/reduce_scatter | solution.py:35
  446.2 0.8 broadcast_multiply_fusion
  446.9 3.2 select_convert_fusion
  450.2 0.8 convolution_convert_fusion
  451.0 0.9 reshape.31
  451.9 0.9 copy.8
  452.8 0.0 all-reduce.5.cloned.1.call-update
  452.8 6.9 %fusion.4 = f32[16,144,32]{1,2,0:T(8,128)S(1)} fusion(bf16[16,144,2048]{2,1,0:T(8,128)(2,1)} %all-gather.2.cloned.1.call-done, bf16[2048,32]{0,1:T(8,128)(2,1)S(1)} %copy-done), kind=kOutput, calls=%fused_computation.10 | convolution fusion | flops 301989888 | bytes 9863168 | tf_op jit(solution)/shard_map/dot_general | solution.py:22
  459.7 129.8 %all-reduce.5.cloned.1.call-done = bf16[16,144,64]{1,2,0:T(8,128)(2,1)} async-done(((bf16[16,144,64]{1,2,0:T(8,128)(2,1)}), bf16[16,144,64]{1,2,0:T(8,128)(2,1)}) %all-reduce.5.cloned.1.call-update) | async-done | bytes 294928 | tf_op jit(solution)/shard_map/psum | solution.py:46
  589.5 1.6 fusion.7
  591.1 0.1 reshape.32
  591.2 0.6 constant_dynamic-slice_fusion
  (9 shorter events, 0.0 us)
Async XLA Ops:
  6.5 446.3 %copy-start = (bf16[2048,32]{0,1:T(8,128)(2,1)S(1)}, bf16[2048,32]{0,1:T(8,128)(2,1)}, u32[]{:S(2)}) copy-start(bf16[2048,32]{0,1:T(8,128)(2,1)} %param.12) | copy-start | bytes 393220
  6.5 229.0 %copy-start.2 = (bf16[16,144,512]{2,1,0:T(8,128)(2,1)S(1)}, bf16[16,144,512]{2,1,0:T(8,128)(2,1)}, u32[]{:S(2)}) copy-start(bf16[16,144,512]{2,1,0:T(8,128)(2,1)} %param.7) | copy-start | bytes 7077892
  6.5 229.0 %all-gather.2.cloned.1.call-start = ((), (), s32[]{:S(2)}) async-start(), calls=%async_computation.2 | async-start | bytes 10027008 | tf_op jit(solution)/shard_map/all_gather | solution.py:19
  7.3 393.8 %all-reduce.3.cloned.1.call-start = ((), (), s32[]{:S(2)}) async-start(), calls=%async_computation.3 | async-start | bytes 2097152 | tf_op jit(solution)/shard_map/psum | solution.py:29
  235.5 18.0 %copy-start.1 = (bf16[512,4096]{1,0:T(8,128)(2,1)S(1)}, bf16[512,4096]{1,0:T(8,128)(2,1)}, u32[]{:S(2)}) copy-start(bf16[512,4096]{1,0:T(8,128)(2,1)} %param.10) | copy-start | bytes 12582916
  246.8 162.9 %copy-start.4 = (s32[64]{0:T(128)S(1)}, s32[64]{0:T(128)}, u32[]{:S(2)}) copy-start(s32[64]{0:T(128)} %param.11) | copy-start | bytes 772
  255.4 190.8 %reduce-scatter.2.cloned.1.call-start = ((), (), s32[]{:S(2)}) async-start(), calls=%async_computation.4 | async-start | bytes 163840 | tf_op jit(solution)/shard_map/reduce_scatter | solution.py:35
  414.3 175.2 %all-reduce.5.cloned.1.call-start = ((), (), s32[]{:S(2)}) async-start(), calls=%async_computation.5 | async-start | bytes 1048576 | tf_op jit(solution)/shard_map/psum | solution.py:46
  446.9 3.2 copy-start.3
Sparse Core Ops, SparseCore 0:
  9.1 226.4 all-gather.1
  255.5 145.4 all-reduce.2
  414.4 31.7 reduce-scatter.1
  452.9 136.4 all-reduce.4
